TPU v7x, 32 devices: a whole 2x2x4 slice. The times are simulated.
32 devices in a mesh: tok: 16 (over z, y, x), head: 2 (over core).
Axes of the slice: x: 2, y: 2, z: 4, core: 2. Of those that a mesh axis runs over, the one named last changes fastest.
Arguments:
- queries: bfloat16 [2, 4096, 512], P('head', 'tok'), may hold values from -6 to 6
- key_rows: bfloat16 [2, 4096, 512], P('head', 'tok'), may hold values from -6 to 6
- value_rows: bfloat16 [2, 4096, 512], P('head', 'tok'), may hold values from -6 to 6
- step_rates: float32 [2, 4096], P('head', 'tok'), may hold values from 0.1 to 1
- w_gate: bfloat16 [2, 512, 512], P('head'), may hold values from -0.25 to 0.25
- w_up: bfloat16 [2, 512, 512], P('head'), may hold values from -0.25 to 0.25
- w_down: bfloat16 [2, 512, 512], P('head'), may hold values from -0.25 to 0.25
- out_gain: float32 [2, 512], P('head'), may hold values from 0.1 to 1.9
- cotangent: bfloat16 [2, 4096, 512], P('head', 'tok'), may hold values from -6 to 6
Outputs:
- grad_queries: bfloat16 [2, 4096, 512], P('head', 'tok')
- grad_keys: bfloat16 [2, 4096, 512], P('head', 'tok')
- grad_values: bfloat16 [2, 4096, 512], P('head', 'tok')
- grad_gate: float32 [2, 512, 512], P('head', 'tok')
- grad_up: float32 [2, 512, 512], P('head', 'tok')
- grad_down: float32 [2, 512, 512], P('head', 'tok')
All inputs are finite; a program needn't handle non-finite values.
Results may differ from a plain program's by a relative error of at most 0.03.
Values sent between devices are 32-bit elements; how exact they have to be, the bound alone decides.
A program may use at most 128 MiB of HBM per device.

v0:
```python
import jax
import jax.numpy as jnp
from jax import lax
from jax.sharding import PartitionSpec as P

NS_STEPS = 3
coef_first = 3.4445
coef_second = -4.775
coef_third = 2.0315
inner_step = 0.5


def contract_rows(first_op, second_op):
    return lax.dot_general(
        first_op, second_op, (((0,), (0,)), ((), ())), preferred_element_type=jnp.float32
    )


def contract_cols(first_op, second_op):
    return lax.dot_general(
        first_op, second_op, (((1,), (1,)), ((), ())), preferred_element_type=jnp.float32
    )


def silu_parts(pre_gate):
    sigma_gate = jax.nn.sigmoid(pre_gate)
    act_gate = pre_gate * sigma_gate
    slope_gate = sigma_gate * (1.0 + pre_gate * (1.0 - sigma_gate))
    return (act_gate, slope_gate, sigma_gate)


def orthogonalize(matrix):
    current = matrix / jnp.sqrt(jnp.sum(matrix * matrix) + 1e-06)
    for iteration in range(NS_STEPS):
        narrow = current.astype(jnp.bfloat16)
        gram_matrix = contract_cols(narrow, narrow)
        gram_low = gram_matrix.astype(jnp.bfloat16)
        poly_term = (
            coef_second * gram_matrix
            + coef_third * jnp.dot(gram_low, gram_low, preferred_element_type=jnp.float32)
        ).astype(jnp.bfloat16)
        current = coef_first * current + jnp.dot(
            poly_term, narrow, preferred_element_type=jnp.float32
        )
    return current


def orthogonalize_all(grad_triple):
    mapped = jax.vmap(orthogonalize)
    return (mapped(grad_triple[0]), mapped(grad_triple[1]), mapped(grad_triple[2]))


def key_forward(w_gate, w_up, w_down, key_rows, value_rows, step_rates):
    key_gate = jnp.dot(key_rows, w_gate, preferred_element_type=jnp.float32)
    key_up = jnp.dot(key_rows, w_up, preferred_element_type=jnp.float32)
    act_gate, slope_gate, sigma_gate = silu_parts(key_gate)
    key_mixed = (act_gate * key_up).astype(jnp.bfloat16)
    target = (-step_rates[:, None] * value_rows).astype(jnp.bfloat16)
    key_mid = contract_cols(target, w_down)
    key_dgate = (key_mid * key_up * slope_gate).astype(jnp.bfloat16)
    key_dup = (key_mid * act_gate).astype(jnp.bfloat16)
    inner_grads = (
        contract_rows(key_rows, key_dgate),
        contract_rows(key_rows, key_dup),
        contract_rows(key_mixed, target),
    )
    stored = (
        key_gate,
        key_up,
        act_gate,
        slope_gate,
        sigma_gate,
        key_mixed,
        target,
        key_mid,
        key_dgate,
        key_dup,
    )
    return (inner_grads, stored)


def key_backward(w_gate, w_up, w_down, key_rows, step_rates, stored, back_a, back_b, back_c):
    (
        key_gate,
        key_up,
        act_gate,
        slope_gate,
        sigma_gate,
        key_mixed,
        target,
        key_mid,
        key_dgate,
        key_dup,
    ) = stored
    cot_a = back_a.astype(jnp.bfloat16)
    cot_b = back_b.astype(jnp.bfloat16)
    cot_c = back_c.astype(jnp.bfloat16)
    back_gate = jnp.dot(key_rows, cot_a, preferred_element_type=jnp.float32)
    back_up = jnp.dot(key_rows, cot_b, preferred_element_type=jnp.float32)
    back_mixed = contract_cols(target, cot_c)
    back_target = jnp.dot(key_mixed, cot_c, preferred_element_type=jnp.float32)
    curve_gate = sigma_gate * (1.0 - sigma_gate) * (2.0 + key_gate * (1.0 - 2.0 * sigma_gate))
    back_mid = (back_gate * key_up * slope_gate + back_up * act_gate).astype(jnp.bfloat16)
    gate_back = (
        back_gate * key_mid * key_up * curve_gate
        + back_up * key_mid * slope_gate
        + back_mixed * key_up * slope_gate
    ).astype(jnp.bfloat16)
    up_back = (back_gate * key_mid * slope_gate + back_mixed * act_gate).astype(jnp.bfloat16)
    key_grad = (
        contract_cols(key_dgate, cot_a)
        + contract_cols(key_dup, cot_b)
        + contract_cols(gate_back, w_gate)
        + contract_cols(up_back, w_up)
    )
    value_sum = back_target + jnp.dot(back_mid, w_down, preferred_element_type=jnp.float32)
    value_grad = (-step_rates[:, None] * value_sum).astype(jnp.bfloat16)
    weight_terms = jnp.concatenate(
        [
            contract_rows(key_rows, gate_back),
            contract_rows(key_rows, up_back),
            contract_rows(back_mid, target),
        ],
        axis=1,
    )
    return (key_grad.astype(jnp.bfloat16), value_grad, weight_terms)


def query_forward(new_gate, new_up, new_down, queries):
    query_gate = jnp.dot(queries, new_gate, preferred_element_type=jnp.float32)
    query_up = jnp.dot(queries, new_up, preferred_element_type=jnp.float32)
    act_gate, slope_gate, sigma_gate = silu_parts(query_gate)
    query_mixed = (act_gate * query_up).astype(jnp.bfloat16)
    output = jnp.dot(query_mixed, new_down, preferred_element_type=jnp.float32)
    return (output, (query_up, act_gate, slope_gate, query_mixed))


def query_backward(new_gate, new_up, new_down, queries, stored, grad_output):
    query_up, act_gate, slope_gate, query_mixed = stored
    query_mid = contract_cols(grad_output, new_down)
    query_dgate = (query_mid * query_up * slope_gate).astype(jnp.bfloat16)
    query_dup = (query_mid * act_gate).astype(jnp.bfloat16)
    query_grad = (contract_cols(query_dgate, new_gate) + contract_cols(query_dup, new_up)).astype(
        jnp.bfloat16
    )
    weight_terms = jnp.concatenate(
        [
            contract_rows(queries, query_dgate),
            contract_rows(queries, query_dup),
            contract_rows(query_mixed, grad_output),
        ],
        axis=1,
    )
    return (query_grad, weight_terms)


def local(queries, key_rows, value_rows, step_rates, w_gate, w_up, w_down, out_gain, cotangent):
    head_size = w_gate.shape[2]
    local_grads, stored = jax.vmap(key_forward)(
        w_gate, w_up, w_down, key_rows, value_rows, step_rates
    )
    inner_grads = lax.psum((local_grads[0], local_grads[1], local_grads[2]), "tok")
    unitary, ns_back = jax.vjp(orthogonalize_all, inner_grads)
    new_gate = (w_gate - inner_step * unitary[0]).astype(jnp.bfloat16)
    new_up = (w_up - inner_step * unitary[1]).astype(jnp.bfloat16)
    new_down = (w_down - inner_step * unitary[2]).astype(jnp.bfloat16)
    output, query_stored = jax.vmap(query_forward)(new_gate, new_up, new_down, queries)
    full_width = queries.shape[0] * lax.axis_size("head") * head_size
    squares_local = jnp.sum(output * output, axis=(0, 2))
    gain_wide = out_gain[:, None, :]
    squares, aligned = lax.psum(
        (squares_local, jnp.sum(cotangent * gain_wide * output, axis=(0, 2))), "head"
    )
    inverse_rms = lax.rsqrt(squares / full_width + 1e-05)
    grad_output = (
        gain_wide * cotangent * inverse_rms[None, :, None]
        - output * (aligned * inverse_rms * inverse_rms * inverse_rms / full_width)[None, :, None]
    ).astype(jnp.bfloat16)
    query_grad, query_terms = jax.vmap(query_backward)(
        new_gate, new_up, new_down, queries, query_stored, grad_output
    )
    share_rows = head_size // lax.axis_size("tok")
    query_whole = lax.psum(query_terms, "tok")
    query_share = lax.dynamic_slice_in_dim(
        query_whole, lax.axis_index("tok") * share_rows, share_rows, 1
    )
    outer_back = (
        -inner_step * query_whole[:, :, :head_size],
        -inner_step * query_whole[:, :, head_size : 2 * head_size],
        -inner_step * query_whole[:, :, 2 * head_size :],
    )
    back_triple = ns_back(outer_back)[0]
    key_grad, value_grad, key_terms = jax.vmap(key_backward)(
        w_gate,
        w_up,
        w_down,
        key_rows,
        step_rates,
        stored,
        back_triple[0],
        back_triple[1],
        back_triple[2],
    )
    key_share = lax.psum_scatter(key_terms, "tok", scatter_dimension=1, tiled=True)
    weight_share = query_share + key_share
    return (
        query_grad,
        key_grad,
        value_grad,
        weight_share[:, :, :head_size],
        weight_share[:, :, head_size : 2 * head_size],
        weight_share[:, :, 2 * head_size :],
    )


def solution(mesh):
    in_specs = (
        P("head", "tok", None),
        P("head", "tok", None),
        P("head", "tok", None),
        P("head", "tok"),
        P("head", None, None),
        P("head", None, None),
        P("head", None, None),
        P("head", None),
        P("head", "tok", None),
    )
    out_specs = (
        P("head", "tok", None),
        P("head", "tok", None),
        P("head", "tok", None),
        P("head", "tok", None),
        P("head", "tok", None),
        P("head", "tok", None),
    )
    return jax.shard_map(local, mesh=mesh, in_specs=in_specs, out_specs=out_specs, check_vma=False)
```

profile of v0, /device:TPU:0, one launch (start us, length us, event | category | flops | bytes accessed | tf_op | source)
XLA Modules:
  0.0 571.0 jit_solution(9727249518634274139)
XLA Ops:
  8.1 1.3 fusion.266
  9.5 1.6 fusion.272
  11.1 2.4 multiply_convert_fusion.2
  13.6 1.3 convolution_bitcast_fusion.8
  14.9 1.4 convolution_bitcast_fusion.7
  16.3 1.4 convolution_bitcast_fusion.6
  21.0 146.9 %all-reduce.11.cloned.1.call-done = (f32[1,512,512]{1,2,0:T(8,128)}, f32[1,512,512]{1,2,0:T(8,128)}, f32[1,512,512]{1,2,0:T(8,128)}) async-done(((f32[1,512,512]{1,2,0:T(8,128)}, f32[1,512,512]{1,2,0:T(8,128)}, f32[1,512,512]{1,2,0:T(8,128)}), (f32[1,512,512]{1,2,0:T(8,128)}, f32[1,512,512]{1,2,0:T(8,128)}, f32[1,512,512]{1,2,0:T(8,128)})) %all-reduce.11.cloned.1.call-update) | async-done | bytes 3145744 | tf_op jit(solution)/shard_map/psum | solution.py:162
  167.9 2.1 multiply_reduce_fusion.5
  170.7 2.2 fusion.263
  176.9 1.3 fusion.26
  184.7 1.2 fusion.29
  198.0 2.5 all-reduce.2
  200.5 1.3 fusion.304
  201.8 1.3 convolution_bitcast_fusion.3
  203.1 1.8 multiply_convert_fusion
  206.0 2.0 pad_maximum_fusion
  208.5 145.7 %all-reduce.7.cloned.1.call-done = f32[1,512,1536]{1,2,0:T(8,128)} async-done(((f32[1,512,1536]{1,2,0:T(8,128)}), f32[1,512,1536]{1,2,0:T(8,128)}) %all-reduce.7.cloned.1.call-update) | async-done | bytes 3145744 | tf_op jit(solution)/shard_map/psum | solution.py:183
  354.2 1.8 convolution_convert_fusion.52
  356.1 1.7 fusion.39
  372.1 1.3 convolution_convert_fusion.22
  381.1 1.3 convolution_convert_fusion.4
  383.9 2.2 multiply_reduce_fusion.2
  386.7 1.9 fusion.49
  388.6 2.0 fusion.103
  391.9 2.1 multiply_reduce_fusion.1
  394.7 3.0 fusion.172
  401.1 1.3 multiply_reduce_fusion
  407.2 5.7 copy.106
  414.8 1.3 fusion.455
  416.1 2.0 fusion.161
  421.6 137.6 %all-reduce.9.cloned.1.call-done = f32[1,512,1536]{2,0,1:T(1,128)} async-done(((f32[1,512,1536]{2,0,1:T(1,128)}), f32[1,512,1536]{2,0,1:T(1,128)}) %all-reduce.9.cloned.1.call-update) | async-done | bytes 3145744
  560.4 1.4 dynamic-slice_add_fusion
  (321 shorter events, 65.7 us)
Async XLA Ops:
  7.2 160.8 %all-reduce.11.cloned.1.call-start = ((), (), s32[]{:S(2)}) async-start(), calls=%async_computation.2 | async-start | bytes 6291456 | tf_op jit(solution)/shard_map/psum | solution.py:162
  9.5 5.4 copy-start.89
  11.1 5.2 copy-start.91
  11.1 5.2 copy-start.46
  13.6 2.7 copy-start.75
  13.6 2.7 copy-start.73
  13.6 2.7 copy-start.77
  14.9 2.9 copy-start.20
  16.3 2.6 copy-start.54
  16.3 3.7 copy-start.29
  17.8 336.4 %all-reduce.7.cloned.1.call-start = ((), (), s32[]{:S(2)}) async-start(), calls=%async_computation | async-start | bytes 6291456 | tf_op jit(solution)/shard_map/psum | solution.py:183
  170.7 2.6 copy-start.33
  193.0 3.1 copy-start.62
  200.5 4.4 copy-start.49
  208.0 351.1 %all-reduce.9.cloned.1.call-start = ((), (), s32[]{:S(2)}) async-start(), calls=%async_computation.1 | async-start | bytes 6291456
  354.2 3.6 copy-start.19
  354.2 4.1 copy-start.1
  354.2 4.1 copy-start.71
  370.9 2.5 copy-start.44
  386.7 4.0 copy-start.102
  394.7 4.2 copy-start.38
  394.7 4.2 copy-start.72
  397.7 2.6 copy-start.24
  412.9 3.2 copy-start.51
  412.9 5.3 copy-start.25
  412.9 5.3 copy-start.78
  412.9 5.6 copy-start.53
  412.9 5.6 copy-start.76
  412.9 5.9 %copy-start.21 = (bf16[1,512,512]{2,1,0:T(8,128)(2,1)S(1)}, bf16[1,512,512]{2,1,0:T(8,128)(2,1)}, u32[]{:S(2)}) copy-start(bf16[1,512,512]{2,1,0:T(8,128)(2,1)} %param.13) | copy-start | bytes 1572868
  414.8 4.0 copy-start.81
  416.1 3.1 copy-start.55
  416.1 3.1 copy-start.87
  (77 other events, 118.6 us)
Sparse Core Ops, SparseCore 0:
  17.9 149.9 all-reduce.10
  208.2 146.0 all-reduce.6
  413.0 146.1 all-reduce.8
where the time goes:
time: 582 us; the launch traced here: 571 us
  waiting for transfers between devices  430 us (74%)
  matrix products  79.5 us (14%)
  local copies, waits for them, and re-layouts  24.8 us (4%)
  between operations  20.8 us (4%)
  other arithmetic  12.9 us (2%)
    psum x1, waiting for transfers between devices, local(): lax.psum((local_grads[0], local_grads[1], local_grads[2]), 'tok')  147 us
    psum x1, waiting for transfers between devices, local(): query_whole = lax.psum(query_terms, 'tok')  146 us
    unnamed x4, waiting for transfers between devices  138 us
    dot_general x36, matrix products, contract_cols(): lax.dot_general(first_op, second_op, (((1,), (1,)), ((), ())), preferred_...  27.5 us
    unnamed x220, local copies, waits for them, and re-layouts  18.8 us
    dot_general x27, matrix products, orthogonalize(): jnp.dot(gram_low, gram_low, preferred_element_type=jnp.float32)  18.8 us
    dot_general x27, matrix products, orthogonalize(): jnp.dot(poly_term, narrow, preferred_element_type=jnp.float32)  17.2 us
  transfers between devices with their start and end apart: 3, of which 3 were waited for; matrix products, arithmetic and copies ran while one was open for 2% of the time, Pallas kernels for 0%

commit v1 on v0

--- a/solution.py
+++ b/solution.py
@@ -8,6 +8,14 @@
 coef_second = -4.775
 coef_third = 2.0315
 inner_step = 0.5
+
+
+def added_up(shard, axis):
+    count, acc = (lax.axis_size(axis), shard)
+    for reach in [1 << k for k in range(count.bit_length() - 1)]:
+        pairs = [(i, i ^ reach) for i in range(count)]
+        acc = acc + lax.ppermute(acc, axis, pairs)
+    return acc
 
 
 def contract_rows(first_op, second_op):
@@ -180,7 +188,7 @@
         new_gate, new_up, new_down, queries, query_stored, grad_output
     )
     share_rows = head_size // lax.axis_size("tok")
-    query_whole = lax.psum(query_terms, "tok")
+    query_whole = added_up(query_terms, "tok")
     query_share = lax.dynamic_slice_in_dim(
         query_whole, lax.axis_index("tok") * share_rows, share_rows, 1
     )

time: 582 us -> 792 us (1.36)
  waiting for transfers between devices: 430 us -> 621 us
    ppermute x0 -> x4, waiting for transfers between devices: none -> 338 us  [added_up(): acc = acc + lax.ppermute(acc, axis, pairs)]
    psum x1 -> x0, waiting for transfers between devices: 146 us -> none  [local(): query_whole = lax.psum(query_terms, 'tok')]
    unnamed x4 -> x3, waiting for transfers between devices: 138 us -> 136 us
  transfers between devices with their start and end apart: 3 -> 6, of which waited for: 3 -> 6; matrix products, arithmetic and copies ran while one was open for 2% -> 2% of each run, Pallas kernels for 0% -> 0%
where the time goes in v1:
time: 792 us; the launch traced here: 781 us
  waiting for transfers between devices  621 us (78%)
  matrix products  78.7 us (10%)
  local copies, waits for them, and re-layouts  31.4 us (4%)
  between operations  21.1 us (3%)
  other arithmetic  19.9 us (3%)
    ppermute x4, waiting for transfers between devices, added_up(): acc = acc + lax.ppermute(acc, axis, pairs)  338 us
    psum x1, waiting for transfers between devices, local(): lax.psum((local_grads[0], local_grads[1], local_grads[2]), 'tok')  147 us
    unnamed x3, waiting for transfers between devices  136 us
    dot_general x36, matrix products, contract_cols(): lax.dot_general(first_op, second_op, (((1,), (1,)), ((), ())), preferred_...  30.5 us
    unnamed x220, local copies, waits for them, and re-layouts  20.7 us
    dot_general x27, matrix products, orthogonalize(): jnp.dot(gram_low, gram_low, preferred_element_type=jnp.float32)  17.5 us
    dot_general x27, matrix products, orthogonalize(): jnp.dot(poly_term, narrow, preferred_element_type=jnp.float32)  15.8 us
  transfers between devices with their start and end apart: 6, of which 6 were waited for; matrix products, arithmetic and copies ran while one was open for 2% of the time, Pallas kernels for 0%

profile of v1, /device:TPU:0, one launch (start us, length us, event | category | flops | bytes accessed | tf_op | source)
XLA Modules:
  0.0 780.9 jit_solution(13507986330791475253)
XLA Ops:
  9.5 1.6 fusion.278
  11.2 2.4 multiply_convert_fusion.2
  16.2 1.4 convolution_bitcast_fusion.6
  20.7 147.1 %all-reduce.8.cloned.1.call-done = (f32[1,512,512]{1,2,0:T(8,128)}, f32[1,512,512]{1,2,0:T(8,128)}, f32[1,512,512]{1,2,0:T(8,128)}) async-done(((f32[1,512,512]{1,2,0:T(8,128)}, f32[1,512,512]{1,2,0:T(8,128)}, f32[1,512,512]{1,2,0:T(8,128)}), (f32[1,512,512]{1,2,0:T(8,128)}, f32[1,512,512]{1,2,0:T(8,128)}, f32[1,512,512]{1,2,0:T(8,128)})) %all-reduce.8.cloned.1.call-update) | async-done | bytes 3145744 | tf_op jit(solution)/shard_map/psum | solution.py:170
  167.8 2.1 multiply_reduce_fusion.5
  170.6 2.2 fusion.269
  199.6 2.6 all-reduce.2
  202.7 1.5 multiply_convert_fusion
  205.2 1.5 collective-permute-start
  206.7 68.7 %collective-permute-done = f32[1,512,1536]{1,2,0:T(8,128)S(1)} collective-permute-done((f32[1,512,1536]{1,2,0:T(8,128)S(1)}, f32[1,512,1536]{1,2,0:T(8,128)S(1)}, u32[]{:S(2)}, u32[]{:S(2)}) %collective-permute-start) | collective-permute-done | bytes 3145760 | tf_op jit(solution)/shard_map/ppermute | solution.py:17
  276.2 1.5 collective-permute-start.1
  277.7 67.8 %collective-permute-done.1 = f32[1,512,1536]{1,2,0:T(8,128)S(1)} collective-permute-done((f32[1,512,1536]{1,2,0:T(8,128)S(1)}, f32[1,512,1536]{1,2,0:T(8,128)S(1)}, u32[]{:S(2)}, u32[]{:S(2)}) %collective-permute-start.1) | collective-permute-done | bytes 3145760 | tf_op jit(solution)/shard_map/ppermute | solution.py:17
  347.2 67.7 %collective-permute-done.2 = f32[1,512,1536]{1,2,0:T(8,128)S(1)} collective-permute-done((f32[1,512,1536]{1,2,0:T(8,128)S(1)}, f32[1,512,1536]{1,2,0:T(8,128)S(1)}, u32[]{:S(2)}, u32[]{:S(2)}) %collective-permute-start.2) | collective-permute-done | bytes 3145760 | tf_op jit(solution)/shard_map/ppermute | solution.py:17
  415.6 1.6 collective-permute-start.3
  417.5 134.2 %collective-permute-done.3 = f32[1,512,1536]{1,2,0:T(8,128)} collective-permute-done((f32[1,512,1536]{1,2,0:T(8,128)S(1)}, f32[1,512,1536]{1,2,0:T(8,128)}, u32[]{:S(2)}, u32[]{:S(2)}) %collective-permute-start.3) | collective-permute-done | bytes 3145760 | tf_op jit(solution)/shard_map/ppermute | solution.py:17
  551.7 3.6 add.198
  583.2 2.1 multiply_reduce_fusion.2
  586.0 2.0 fusion.49
  588.0 2.0 fusion.103
  591.2 2.1 multiply_reduce_fusion.1
  594.0 3.7 fusion.166
  601.1 2.1 multiply_reduce_fusion
  603.9 2.0 fusion.168
  605.9 1.5 fusion.196
  609.5 1.9 pad_maximum_fusion.1
  611.4 8.6 %copy.106 = f32[1,512,1536]{2,0,1:T(1,128)} copy(f32[1,512,1536]{1,2,0:T(8,128)} %pad_maximum_fusion.1) | data formatting | bytes 6291456 | tf_op jit(solution)/shard_map/vmap()/concatenate | solution.py:126
  621.9 1.6 fusion.462
  623.5 2.3 fusion.155
  630.3 135.9 %all-reduce.6.cloned.1.call-done = f32[1,512,1536]{2,0,1:T(1,128)} async-done(((f32[1,512,1536]{2,0,1:T(1,128)}), f32[1,512,1536]{2,0,1:T(1,128)}) %all-reduce.6.cloned.1.call-update) | async-done | bytes 3145744
  766.2 1.6 constant_dynamic-slice_fusion
  767.8 2.1 copy.107
  769.9 1.4 dynamic-slice_add_fusion
  (330 shorter events, 79.3 us)
Async XLA Ops:
  7.2 160.6 %all-reduce.8.cloned.1.call-start = ((), (), s32[]{:S(2)}) async-start(), calls=%async_computation.1 | async-start | bytes 6291456 | tf_op jit(solution)/shard_map/psum | solution.py:170
  9.5 5.4 copy-start.90
  11.1 5.0 copy-start.92
  11.1 5.1 copy-start.52
  16.2 3.5 copy-start.33
  17.6 748.6 %all-reduce.6.cloned.1.call-start = ((), (), s32[]{:S(2)}) async-start(), calls=%async_computation | async-start | bytes 6291456
  170.6 3.7 copy-start.38
  177.3 18.1 %copy-start.5 = (f32[1,512,512]{1,2,0:T(8,128)}, f32[1,512,512]{1,2,0:T(8,128)S(1)}, u32[]{:S(2)}) copy-start(f32[1,512,512]{1,2,0:T(8,128)S(1)} %fusion.10) | copy-start | bytes 3145732
  186.1 10.3 %copy-start.3 = (f32[1,512,512]{1,2,0:T(8,128)}, f32[1,512,512]{1,2,0:T(8,128)S(1)}, u32[]{:S(2)}) copy-start(f32[1,512,512]{1,2,0:T(8,128)S(1)} %fusion.15) | copy-start | bytes 3145732
  194.4 4.0 copy-start.1
  205.2 70.2 %collective-permute-start = (f32[1,512,1536]{1,2,0:T(8,128)S(1)}, f32[1,512,1536]{1,2,0:T(8,128)S(1)}, u32[]{:S(2)}, u32[]{:S(2)}) collective-permute-start(f32[1,512,1536]{1,2,0:T(8,128)S(1)} %pad_maximum_fusion), channel_id=1, source_target_pairs={{0,2},{2,0},{4,6},{6,4},{8,10},{10,8},{12,14},{14,12},{16,18},{18,... | collective-permute-start | bytes 9437192 | tf_op jit(solution)/shard_map/ppermute | solution.py:17
  276.2 69.4 %collective-permute-start.1 = (f32[1,512,1536]{1,2,0:T(8,128)S(1)}, f32[1,512,1536]{1,2,0:T(8,128)S(1)}, u32[]{:S(2)}, u32[]{:S(2)}) collective-permute-start(f32[1,512,1536]{1,2,0:T(8,128)S(1)} %fusion.409), channel_id=1, source_target_pairs={{0,4},{2,6},{4,0},{6,2},{8,12},{10,14},{12,8},{14,10},{16,20},{18,... | collective-permute-start | bytes 9437192 | tf_op jit(solution)/shard_map/ppermute | solution.py:17
  346.3 68.5 %collective-permute-start.2 = (f32[1,512,1536]{1,2,0:T(8,128)S(1)}, f32[1,512,1536]{1,2,0:T(8,128)S(1)}, u32[]{:S(2)}, u32[]{:S(2)}) collective-permute-start(f32[1,512,1536]{1,2,0:T(8,128)S(1)} %add.196), channel_id=1, source_target_pairs={{0,8},{2,10},{4,12},{6,14},{8,0},{10,2},{12,4},{14,6},{16,24},{18,... | collective-permute-start | bytes 9437192 | tf_op jit(solution)/shard_map/ppermute | solution.py:17
  415.6 136.1 %collective-permute-start.3 = (f32[1,512,1536]{1,2,0:T(8,128)S(1)}, f32[1,512,1536]{1,2,0:T(8,128)}, u32[]{:S(2)}, u32[]{:S(2)}) collective-permute-start(f32[1,512,1536]{1,2,0:T(8,128)S(1)} %add.197), channel_id=1, source_target_pairs={{0,16},{2,18},{4,20},{6,22},{8,24},{10,26},{12,28},{14,30},{16,0},... | collective-permute-start | bytes 9437192 | tf_op jit(solution)/shard_map/ppermute | solution.py:17
  417.5 137.8 %copy-start.6 = (f32[1,512,512]{1,2,0:T(8,128)S(1)}, f32[1,512,512]{1,2,0:T(8,128)}, u32[]{:S(2)}) copy-start(f32[1,512,512]{1,2,0:T(8,128)} %copy-done.5) | copy-start | bytes 3145732
  585.9 4.0 copy-start.42
  585.9 4.0 copy-start.102
  594.0 4.8 copy-start.44
  594.0 4.8 copy-start.75
  603.9 3.5 copy-start.62
  603.9 3.5 copy-start.91
  603.9 3.5 copy-start.93
  603.9 3.5 copy-start.94
  603.9 3.5 copy-start.105
  621.9 3.9 copy-start.30
  621.9 5.3 copy-start.63
  621.9 5.3 copy-start.79
  621.9 5.6 copy-start.27
  621.9 5.6 copy-start.83
  623.5 4.4 copy-start.65
  623.5 4.4 copy-start.89
  625.8 3.1 copy-start.77
  (80 other events, 131.5 us)
Sparse Core Ops, SparseCore 0:
  17.7 149.9 all-reduce.7
  620.1 146.0 all-reduce.5
